TPU v7x, 32 devices: a whole 2x2x4 slice. The times are simulated.
32 devices in a mesh: tm: 8 (over z, y), state: 4 (over x, core).
Axes of the slice: x: 2, y: 2, z: 4, core: 2. Of those that a mesh axis runs over, the one named last changes fastest.
Arguments:
- jacobian: bfloat16 [256, 64, 1024], P('tm', None, 'state'), may hold values from -0.125 to 0.125
- measurement: float32 [256, 64], P('tm'), may hold values from -6 to 6
- depth_block: int32 [256], P('tm'), may hold values from 0 to 4799
- precision: float32 [4800], replicated, may hold values from 0.25 to 4
- valid_slot_counts: int32 [8], P('tm'), may hold values from 10 to 32, as said below
- retention: float32 [40, 1024], P('tm'), may hold values from 0.45 to 1, as said below
Outputs:
- info_diagonal: float32 [8192], P(('tm', 'state'))
- info_vector: float32 [8192], P(('tm', 'state'))
- final_info: float32 [1024, 1024], P('state', 'tm')
Inputs may be any that keep to these rules, and one draw needn't show every extreme that they name: `valid_slot_counts`: each frame block has at least 10 and at most 32 valid slots; in every draw some block has exactly 32 and some exactly 10. `retention`: every factor is positive and at most one.
All inputs are finite; a program needn't handle non-finite values.
Results may differ from a plain program's by a relative error of at most 0.0039.
Values may be sent and summed in bfloat16 or wider, within the bound.
A program may use at most 64 MiB of HBM per device.

v0:
```python
import jax
import jax.numpy as jnp
from jax import lax
from jax.sharding import PartitionSpec as P


def local_tables(block_forget_factor, active_slot_count, depth_row_index, precision, n_slots):
    frame_total = block_forget_factor.shape[0]
    backward = jnp.flip(jnp.cumprod(jnp.flip(block_forget_factor, 0), 0), 0)
    through = backward[0]
    kept = jnp.concatenate(
        [backward[1:], jnp.ones((1, block_forget_factor.shape[1]), block_forget_factor.dtype)], 0
    )
    slot_ids = jnp.arange(n_slots, dtype=jnp.int32)
    frames = slot_ids * frame_total // active_slot_count
    onehot = (frames[:, None] == jnp.arange(frame_total, dtype=jnp.int32)[None, :]).astype(
        block_forget_factor.dtype
    )
    colfac = jnp.dot(onehot, kept, precision=lax.Precision.HIGHEST)
    matches = depth_row_index[:, None] == jnp.arange(precision.shape[0], dtype=jnp.int32)[None, :]
    picked = jnp.sum(jnp.where(matches, precision[None, :], 0.0), axis=1)
    row_multiplier = jnp.where(slot_ids < active_slot_count, jnp.sqrt(picked), 0.0)
    return (through, colfac, row_multiplier)


def scale_blocks(block_jacobian_matrix, row_multiplier, colfac):
    scaled = (
        block_jacobian_matrix.astype(jnp.float32)
        * row_multiplier[:, None, None]
        * colfac[:, None, :]
    )
    return scaled.astype(jnp.bfloat16).reshape(-1, block_jacobian_matrix.shape[2])


def gram_slab(block_jacobian_matrix, row_multiplier, colfac, row_start, row_count):
    scaled = scale_blocks(block_jacobian_matrix, row_multiplier, colfac)
    left_cols = lax.dynamic_slice_in_dim(scaled, row_start, row_count, 1)
    return lax.dot_general(
        left_cols, scaled, (((0,), (0,)), ((), ())), preferred_element_type=jnp.float32
    )


def local(jacobian, measurement, depth_block, precision, valid_slot_counts, retention):
    n_slots = jacobian.shape[0]
    stripe_width = jacobian.shape[2]
    stripes = lax.axis_size("state")
    stripe = lax.axis_index("state")
    position = lax.axis_index("tm")
    full_width = stripe_width * stripes
    active_slot_count = valid_slot_counts[0]
    through, colfac, row_multiplier = local_tables(
        retention, active_slot_count, depth_block, precision, n_slots
    )
    own_colfac = lax.dynamic_slice_in_dim(colfac, stripe * stripe_width, stripe_width, 1)
    local_scaled = scale_blocks(jacobian, row_multiplier, own_colfac)
    weighted_jacobian = (measurement * row_multiplier[:, None]).astype(jnp.bfloat16).reshape(-1)
    own_vector = jnp.dot(weighted_jacobian, local_scaled, preferred_element_type=jnp.float32)
    whole_jac = lax.all_gather(jacobian, "state", axis=2, tiled=True)
    gram_rows = gram_slab(whole_jac, row_multiplier, colfac, stripe * stripe_width, stripe_width)
    own_block = lax.dynamic_slice_in_dim(gram_rows, stripe * stripe_width, stripe_width, 1)
    own_diagonal = jnp.diagonal(own_block)

    def combine(earlier, later):
        later_rows = lax.dynamic_slice_in_dim(
            later[0], stripe * stripe_width, stripe_width, later[0].ndim - 1
        )
        product = earlier[0] * later[0]
        diag_next = later_rows * later_rows * earlier[1] + later[1]
        vec_next = later_rows * earlier[2] + later[2]
        return (product, diag_next, vec_next)

    all_through, all_diagonal, all_vector = (
        lax.all_gather(through[None, :], "tm", axis=0, tiled=True),
        lax.all_gather(own_diagonal[None, :], "tm", axis=0, tiled=True),
        lax.all_gather(own_vector[None, :], "tm", axis=0, tiled=True),
    )
    running = lax.associative_scan(combine, (all_through, all_diagonal, all_vector), axis=0)
    info_diagonal = lax.dynamic_index_in_dim(running[1], position, 0, keepdims=False)
    info_vector = lax.dynamic_index_in_dim(running[2], position, 0, keepdims=False)
    backward_decay = jnp.flip(jnp.cumprod(jnp.flip(all_through, 0), 0), 0)
    padded_decay = jnp.concatenate([backward_decay, jnp.ones((1, full_width), jnp.float32)], 0)
    later_weight = lax.dynamic_index_in_dim(padded_decay, position + 1, 0, keepdims=False)
    later_stripe = lax.dynamic_slice_in_dim(later_weight, stripe * stripe_width, stripe_width, 0)
    decayed_rows = later_stripe[:, None] * gram_rows * later_weight[None, :]
    final_info = lax.psum_scatter(decayed_rows, "tm", scatter_dimension=1, tiled=True)
    return (info_diagonal, info_vector, final_info)


def solution(mesh):
    in_specs = (P("tm", None, "state"), P("tm", None), P("tm"), P(), P("tm"), P("tm", None))
    out_specs = (P(("tm", "state")), P(("tm", "state")), P("state", "tm"))
    return jax.shard_map(local, mesh=mesh, in_specs=in_specs, out_specs=out_specs, check_vma=False)
```

profile of v0, /device:TPU:0, one launch (start us, length us, event | category | flops | bytes accessed | tf_op | source)
XLA Modules:
  0.0 144.2 jit_solution(5366735744313004321)
XLA Ops:
  7.2 0.0 all-gather.7.cloned.1.call-start
  7.2 0.7 all-gather.7.cloned.1.call-update
  7.9 0.0 reduce-scatter.2.cloned.1.call-start
  8.0 2.8 %rev.12 = f32[5,1024]{1,0:T(8,128)S(1)} reverse(f32[5,1024]{1,0:T(8,128)} %param.11), dimensions={0} | reverse | bytes 40960 | tf_op jit(solution)/shard_map/jit(_flip)/rev | solution.py:9
  11.5 0.2 slice.114
  11.7 0.1 and_select_fusion
  11.8 0.2 fusion.4
  12.1 1.0 select_reduce_fusion
  13.1 0.8 fusion.7
  13.9 1.7 %convolution_bitcast_fusion = f32[1,1,256]{2,1,0:T(1,128)S(1)} fusion(bf16[32,64,256]{2,1,0:T(8,128)(2,1)} %param.6, f32[32,256]{1,0:T(8,128)S(1)} %constant_dynamic-slice_fusion.4, f32[32]{0:T(128)S(1)} %compare_select_fusion, bf16[32,64,1]{1,0,2:T(8,128)(2,1)S(1)} %fusion.7), kind=kOutput, calls=%fused_computation.3 | convolution fusion | flops 3145728 | bytes 1086592 | tf_op jit(solution)/shard_map/dot_general | solution.py:57
  15.5 22.3 %all-gather.4 = f32[8,1,256]{2,1,0:T(1,128)S(1)} all-gather(f32[1,1,256]{2,1,0:T(1,128)S(1)} %convolution_bitcast_fusion), channel_id=3, replica_groups=mesh['tm'=8,'state'=4] {'tm'}, dimensions={0}, use_global_device_ids=true | all-gather | bytes 9216 | tf_op jit(solution)/shard_map/all_gather | solution.py:75
  37.9 30.6 %all-gather.3 = f32[8,1,1024]{2,1,0:T(1,128)S(1)} all-gather(f32[1,1,1024]{2,1,0:T(1,128)S(1)} %slice_bitcast_fusion), channel_id=1, replica_groups=mesh['tm'=8,'state'=4] {'tm'}, dimensions={0}, use_global_device_ids=true | all-gather | bytes 36864 | tf_op jit(solution)/shard_map/all_gather | solution.py:73
  68.5 0.2 rev.13
  68.9 0.2 rev.14
  69.1 0.1 pad_dynamic-slice_fusion.1
  69.2 0.0 all-gather.7.cloned.1.call-done
  69.2 3.8 %multiply_convert_fusion = bf16[32,64,1024]{2,1,0:T(8,128)(2,1)S(1)} fusion(bf16[32,64,1024]{2,1,0:T(8,128)(2,1)} %all-gather.7.cloned.1.call-done, f32[32,1024]{1,0:T(8,128)S(1)} %fusion.4, f32[32]{0:T(128)S(1)} %compare_select_fusion), kind=kLoop, calls=%fused_computation.1 | loop fusion | flops 8388608 | bytes 8519808 | tf_op jit(solution)/shard_map/convert_element_type | solution.py:32
  73.0 2.3 %multiply_multiply_fusion = (f32[256,1024]{1,0:T(8,128)}, f32[256,1024]{1,0:T(8,128)S(1)}) fusion(f32[1024]{0:T(1024)S(1)} %bitcast.45, f32[256]{0:T(256)S(1)} %bitcast.48, bf16[2048,1024]{1,0:T(8,128)(2,1)S(1)} %bitcast.34, s32[]{:T(128)S(6)} %select_n.56), kind=kOutput, calls=%fused_computation.4 | convolution fusion | flops 1074266112 | bytes 7345156 | tf_op jit(solution)/shard_map/dot_general | solution.py:38
  75.3 0.0 reduce-scatter.2.cloned.1.call-update
  75.4 2.3 %gather_fusion = f32[256]{0:T(256)S(1)} fusion(f32[256,256]{1,0:T(8,128)S(1)} %constant_dynamic-slice_fusion.11, s32[256]{0:T(256)S(1)} %bitcast.33), kind=kCustom, calls=%fused_computation | custom fusion | bytes 4096 | tf_op jit(solution)/shard_map/jit(diagonal)/cond/branch_0_fun/gather | solution.py:61
  77.7 16.3 %all-gather.2 = f32[8,1,256]{2,1,0:T(1,128)S(1)} all-gather(f32[1,1,256]{2,1,0:T(1,128)S(1)} %bitcast.46), channel_id=2, replica_groups=mesh['tm'=8,'state'=4] {'tm'}, dimensions={0}, use_global_device_ids=true | all-gather | bytes 9216 | tf_op jit(solution)/shard_map/all_gather | solution.py:74
  94.5 0.6 fusion.18
  95.0 0.6 fusion.17
  95.6 41.8 %reduce-scatter.2.cloned.1.call-done = f32[256,128]{1,0:T(8,128)} async-done(((f32[256,1024]{1,0:T(8,128)}), f32[256,128]{1,0:T(8,128)}) %reduce-scatter.2.cloned.1.call-update) | async-done | bytes 131088 | tf_op jit(solution)/shard_map/reduce_scatter | solution.py:85
  (52 shorter events, 0.8 us)
Async XLA Ops:
  7.2 62.1 %all-gather.7.cloned.1.call-start = ((), (), s32[]{:S(2)}) async-start(), calls=%async_computation.1 | async-start | bytes 5242880 | tf_op jit(solution)/shard_map/all_gather | solution.py:58
  7.9 129.5 %reduce-scatter.2.cloned.1.call-start = ((), (), s32[]{:S(2)}) async-start(), calls=%async_computation.2 | async-start | bytes 1179648 | tf_op jit(solution)/shard_map/reduce_scatter | solution.py:85
Sparse Core Ops, SparseCore 0:
  9.5 37.7 all-gather.6
  75.5 61.9 reduce-scatter.1
where the time goes:
time: 145 us; the launch traced here: 144 us
  blocking collectives  69.2 us (48%)
  waiting for transfers between devices  42.5 us (29%)
  between operations  14.9 us (10%)
  other arithmetic  7.03 us (5%)
  local copies, waits for them, and re-layouts  6.31 us (4%)
  matrix products  4.18 us (3%)
    reduce_scatter x1, waiting for transfers between devices, local(): lax.psum_scatter(decayed_rows, 'tm', scatter_dimension=1, tiled=True)  41.8 us
    all_gather x1, blocking collectives, local(): lax.all_gather(through[None, :], 'tm', axis=0, tiled=True)  30.6 us
    all_gather x1, blocking collectives, local(): lax.all_gather(own_vector[None, :], 'tm', axis=0, tiled=True)  22.3 us
    all_gather x1, blocking collectives, local(): lax.all_gather(own_diagonal[None, :], 'tm', axis=0, tiled=True)  16.3 us
    convert_element_type x1, other arithmetic, scale_blocks(): scaled.astype(jnp.bfloat16).reshape(-1, block_jacobian_matrix.shape[2])  3.79 us
  transfers between devices with their start and end apart: 2, of which 1 were waited for; matrix products, arithmetic and copies ran while one was open for 8% of the time, Pallas kernels for 0%

commit v1 on v0

--- a/solution.py
+++ b/solution.py
@@ -1,6 +1,9 @@
+import functools
 import jax
 import jax.numpy as jnp
 from jax import lax
+from jax.experimental import pallas as pl
+from jax.experimental.pallas import tpu as pltpu
 from jax.sharding import PartitionSpec as P
 
 
@@ -86,7 +89,319 @@
     return (info_diagonal, info_vector, final_info)
 
 
+MESH = pl.DeviceIdType.MESH
+LANES = 128
+GROUP = 8
+
+
+def filter_kernel(
+    n_tm,
+    jac,
+    meas,
+    depth,
+    prec,
+    live,
+    ret,
+    diag_out,
+    vec_out,
+    info_out,
+    partner_jac,
+    across_jac,
+    relay_jac,
+    weight,
+    own_t,
+    small,
+    later,
+    row_decay,
+    outgoing,
+    incoming,
+    jac_send,
+    jac_recv,
+    small_send,
+    small_recv,
+    gram_send,
+    gram_recv,
+):
+    t = lax.axis_index("tm")
+    s = lax.axis_index("state")
+    x = s // 2
+    c = s % 2
+    partner = (t, x * 2 + 1 - c)
+    across = (t, (1 - x) * 2 + c)
+    n_slots, n_rows, width = jac.shape
+    n_frames, full = ret.shape
+    stripes = full // width
+    groups = n_slots // GROUP
+    depth_rows = GROUP * n_rows
+
+    barrier = pltpu.get_barrier_semaphore()
+    for device in (partner, across):
+        pl.semaphore_signal(barrier, inc=1, device_id=device, device_id_type=MESH)
+    for step in range(1, n_tm):
+        pl.semaphore_signal(
+            barrier, inc=1, device_id=(lax.rem(t + step, n_tm), s), device_id_type=MESH
+        )
+    pl.semaphore_wait(barrier, n_tm + 1)
+
+    def lanes(half):
+        return pl.ds(pl.multiple_of(half * LANES, LANES), LANES)
+
+    def cross_copy(phase):
+        half = lax.rem(c + phase, 2)
+        return pltpu.make_async_remote_copy(
+            src_ref=jac.at[:, :, lanes(half)],
+            dst_ref=across_jac.at[phase],
+            send_sem=jac_send.at[phase],
+            recv_sem=jac_recv.at[phase],
+            device_id=across,
+            device_id_type=MESH,
+        )
+
+    def relay_copy(phase):
+        return pltpu.make_async_remote_copy(
+            src_ref=across_jac.at[phase],
+            dst_ref=relay_jac.at[phase],
+            send_sem=jac_send.at[2 + phase],
+            recv_sem=jac_recv.at[2 + phase],
+            device_id=partner,
+            device_id_type=MESH,
+        )
+
+    partner_copy = pltpu.make_async_remote_copy(
+        src_ref=jac,
+        dst_ref=partner_jac,
+        send_sem=jac_send.at[4],
+        recv_sem=jac_recv.at[4],
+        device_id=partner,
+        device_id_type=MESH,
+    )
+    cross_copy(0).start()
+    cross_copy(1).start()
+    partner_copy.start()
+
+    active = live[0]
+    slot_col = lax.broadcasted_iota(jnp.int32, (n_slots, 1), 0)
+    eye = lax.broadcasted_iota(jnp.int32, (n_slots, n_slots), 0) == lax.broadcasted_iota(
+        jnp.int32, (n_slots, n_slots), 1
+    )
+    depth_col = jnp.sum(
+        jnp.where(eye, jnp.broadcast_to(depth[...], (n_slots, n_slots)), 0), axis=1, keepdims=True
+    )
+    picks = depth_col == lax.broadcasted_iota(jnp.int32, (n_slots, prec.shape[1]), 1)
+    picked = jnp.sum(jnp.where(picks, prec[...], 0.0), axis=1, keepdims=True)
+    row_weight = jnp.where(slot_col < active, jnp.sqrt(picked), 0.0)
+    factor = ret[pl.ds(n_frames - 1, 1), :]
+    colfac = jnp.ones((n_slots, full), jnp.float32)
+    for frame in range(n_frames - 2, -1, -1):
+        colfac = jnp.where(slot_col * n_frames < (frame + 1) * active, factor, colfac)
+        factor = factor * ret[pl.ds(frame, 1), :]
+    weight[...] = row_weight * colfac
+    measured = (meas[...] * row_weight).astype(jnp.bfloat16)
+
+    def scaled_parts(ref, g, column, count):
+        first = pl.multiple_of(g * GROUP, GROUP)
+        weights = weight[pl.ds(first, GROUP), pl.ds(column, count)]
+        return [
+            (ref[first + i].astype(jnp.float32) * weights[i : i + 1, :]).astype(jnp.bfloat16)
+            for i in range(GROUP)
+        ]
+
+    own_column = pl.multiple_of(s * width, width)
+
+    def own_step(g, carry):
+        squares, vector = carry
+        parts = scaled_parts(jac, g, own_column, width)
+        for i, part in enumerate(parts):
+            wide = part.astype(jnp.float32)
+            squares = squares + jnp.sum(
+                (wide * wide).reshape(n_rows // 8, 8, width), axis=0
+            )
+            hit = jnp.dot(measured, part, preferred_element_type=jnp.float32)
+            vector = vector + jnp.where(slot_col == g * GROUP + i, hit, 0.0)
+        block = jnp.concatenate(parts, axis=0)
+        own_t[:, pl.ds(pl.multiple_of(g * depth_rows, depth_rows), depth_rows)] = block.T
+        return squares, vector
+
+    squares, vector = lax.fori_loop(
+        0,
+        groups,
+        own_step,
+        (jnp.zeros((8, width), jnp.float32), jnp.zeros((n_slots, width), jnp.float32)),
+    )
+    rows = [factor[:, q * width : (q + 1) * width] for q in range(stripes)]
+    rows.append(jnp.sum(squares, axis=0, keepdims=True))
+    rows.append(jnp.sum(vector, axis=0, keepdims=True))
+    rows.append(jnp.zeros((8 - len(rows), width), jnp.float32))
+    small[t] = jnp.concatenate(rows, axis=0)
+
+    def small_copy(source, target):
+        return pltpu.make_async_remote_copy(
+            src_ref=small.at[source],
+            dst_ref=small.at[source],
+            send_sem=small_send.at[target],
+            recv_sem=small_recv.at[source],
+            device_id=(target, s),
+            device_id_type=MESH,
+        )
+
+    for step in range(1, n_tm):
+        small_copy(t, lax.rem(t + step, n_tm)).start()
+
+    def gram_chunk(ref, column):
+        def body(g, total):
+            block = jnp.concatenate(scaled_parts(ref, g, column, LANES), axis=0)
+            rows = pl.ds(pl.multiple_of(g * depth_rows, depth_rows), depth_rows)
+            return total + jnp.dot(own_t[:, rows], block, preferred_element_type=jnp.float32)
+
+        return lax.fori_loop(0, groups, body, jnp.zeros((width, LANES), jnp.float32))
+
+    def gram_copy(source, target):
+        return pltpu.make_async_remote_copy(
+            src_ref=outgoing.at[target],
+            dst_ref=incoming.at[source],
+            send_sem=gram_send.at[target],
+            recv_sem=gram_recv.at[source],
+            device_id=(target, s),
+            device_id_type=MESH,
+        )
+
+    def send_chunk(gram, stripe, half):
+        chunk = stripe * 2 + half
+        decay = later[stripe, pl.ds(0, 1), lanes(half)]
+        outgoing[chunk] = (gram * row_decay[...] * decay).astype(jnp.bfloat16)
+
+        @pl.when(chunk != t)
+        def _():
+            gram_copy(t, chunk).start()
+
+    own_grams = [
+        gram_chunk(jac.at[:, :, lanes(half)], pl.multiple_of(s * width + half * LANES, LANES))
+        for half in range(2)
+    ]
+
+    for step in range(1, n_tm):
+        source = lax.rem(t + step, n_tm)
+        small_copy(source, source).wait_recv()
+
+    def own_row(values):
+        mine = lax.broadcasted_iota(jnp.int32, (stripes, width), 0) == s
+        return jnp.sum(jnp.where(mine, values, 0.0), axis=0, keepdims=True)
+
+    product = jnp.ones((stripes, width), jnp.float32)
+    diagonal = jnp.zeros((1, width), jnp.float32)
+    info = jnp.zeros((1, width), jnp.float32)
+    for block in range(n_tm):
+        message = small[block]
+        throughs = message[:stripes, :]
+        product = jnp.where(block > t, product * throughs, product)
+        through = own_row(throughs)
+        more_diagonal = through * through * diagonal + message[stripes : stripes + 1, :]
+        more_info = through * info + message[stripes + 1 : stripes + 2, :]
+        diagonal = jnp.where(block <= t, more_diagonal, diagonal)
+        info = jnp.where(block <= t, more_info, info)
+    diag_out[...] = diagonal
+    vec_out[...] = info
+    for q in range(stripes):
+        later[q] = jnp.broadcast_to(product[q : q + 1, :], (8, width))
+    row_decay[...] = jnp.broadcast_to(own_row(product), (LANES, width)).T
+
+    for half in range(2):
+        send_chunk(own_grams[half], s, half)
+    partner_copy.wait_recv()
+    other = x * 2 + 1 - c
+    for half in range(2):
+        send_chunk(
+            gram_chunk(
+                partner_jac.at[:, :, lanes(half)],
+                pl.multiple_of(other * width + half * LANES, LANES),
+            ),
+            other,
+            half,
+        )
+    near = (1 - x) * 2 + c
+    far = (1 - x) * 2 + 1 - c
+    for phase in range(2):
+        cross_copy(phase).wait_recv()
+        relay_copy(phase).start()
+        half = lax.rem(c + phase, 2)
+        column = pl.multiple_of(near * width + half * LANES, LANES)
+        send_chunk(gram_chunk(across_jac.at[phase], column), near, half)
+        relay_copy(phase).wait_recv()
+        half = lax.rem(1 - c + phase, 2)
+        column = pl.multiple_of(far * width + half * LANES, LANES)
+        send_chunk(gram_chunk(relay_jac.at[phase], column), far, half)
+
+    total = outgoing[t].astype(jnp.float32)
+    for step in range(1, n_tm):
+        source = lax.rem(t + step, n_tm)
+        gram_copy(source, source).wait_recv()
+        total = total + incoming[source].astype(jnp.float32)
+    info_out[...] = total
+
+    for step in range(1, n_tm):
+        target = lax.rem(t + step, n_tm)
+        gram_copy(t, target).wait_send()
+        small_copy(t, target).wait_send()
+    partner_copy.wait_send()
+    for phase in range(2):
+        cross_copy(phase).wait_send()
+        relay_copy(phase).wait_send()
+
+
+def fused(n_tm, jacobian, measurement, depth_block, precision, valid_slot_counts, retention):
+    n_slots, n_rows, width = jacobian.shape
+    full = retention.shape[1]
+    stripes = full // width
+    vmem = pl.BlockSpec(memory_space=pltpu.VMEM)
+    diagonal, vector, info = pl.pallas_call(
+        functools.partial(filter_kernel, n_tm),
+        out_shape=(
+            jax.ShapeDtypeStruct((1, width), jnp.float32),
+            jax.ShapeDtypeStruct((1, width), jnp.float32),
+            jax.ShapeDtypeStruct((width, LANES), jnp.float32),
+        ),
+        in_specs=[vmem] * 4 + [pl.BlockSpec(memory_space=pltpu.SMEM), vmem],
+        out_specs=(vmem, vmem, vmem),
+        scratch_shapes=[
+            pltpu.VMEM((n_slots, n_rows, width), jnp.bfloat16),
+            pltpu.VMEM((2, n_slots, n_rows, LANES), jnp.bfloat16),
+            pltpu.VMEM((2, n_slots, n_rows, LANES), jnp.bfloat16),
+            pltpu.VMEM((n_slots, full), jnp.float32),
+            pltpu.VMEM((width, n_slots * n_rows), jnp.bfloat16),
+            pltpu.VMEM((n_tm, 8, width), jnp.float32),
+            pltpu.VMEM((stripes, 8, width), jnp.float32),
+            pltpu.VMEM((width, LANES), jnp.float32),
+            pltpu.VMEM((n_tm, width, LANES), jnp.bfloat16),
+            pltpu.VMEM((n_tm, width, LANES), jnp.bfloat16),
+            pltpu.SemaphoreType.DMA((5,)),
+            pltpu.SemaphoreType.DMA((5,)),
+            pltpu.SemaphoreType.DMA((n_tm,)),
+            pltpu.SemaphoreType.DMA((n_tm,)),
+            pltpu.SemaphoreType.DMA((n_tm,)),
+            pltpu.SemaphoreType.DMA((n_tm,)),
+        ],
+        compiler_params=pltpu.CompilerParams(collective_id=0, has_side_effects=True),
+    )(
+        jacobian,
+        measurement,
+        depth_block[None, :],
+        precision[None, :],
+        valid_slot_counts,
+        retention,
+    )
+    return diagonal.reshape(width), vector.reshape(width), info
+
+
 def solution(mesh):
+    n_tm, stripes = mesh.shape["tm"], mesh.shape["state"]
+
+    def body(jacobian, measurement, depth_block, precision, valid_slot_counts, retention):
+        args = (jacobian, measurement, depth_block, precision, valid_slot_counts, retention)
+        n_slots, _, width = jacobian.shape
+        if stripes == 4 and width == 2 * LANES and n_tm * LANES == width * stripes and n_slots % GROUP == 0:
+            return fused(n_tm, *args)
+        return local(*args)
+
     in_specs = (P("tm", None, "state"), P("tm", None), P("tm"), P(), P("tm"), P("tm", None))
     out_specs = (P(("tm", "state")), P(("tm", "state")), P("state", "tm"))
-    return jax.shard_map(local, mesh=mesh, in_specs=in_specs, out_specs=out_specs, check_vma=False)
+    return jax.shard_map(body, mesh=mesh, in_specs=in_specs, out_specs=out_specs, check_vma=False)

time: 145 us -> 45.4 us (0.31)
  the two profiles are of different devices: /device:TPU:0 before, /device:TPU:7 now
where the time goes in v1:
time: 45.4 us; the launch traced here: 45.1 us
  Pallas kernels  39 us (86%)
  local copies, waits for them, and re-layouts  4.77 us (11%)
  between operations  1.3 us (3%)
    pallas_call x1, Pallas kernels, fused(): pl.pallas_call(functools.partial(filter_kernel, n_tm), out_shape=(jax.Sha...  39 us
    unnamed x7, local copies, waits for them, and re-layouts  3.42 us
    broadcast_in_dim x1, local copies, waits for them, and re-layouts, fused(): precision[None, :]  1.35 us

profile of v1, /device:TPU:7, one launch (start us, length us, event | category | flops | bytes accessed | tf_op | source)
XLA Modules:
  0.0 45.1 jit_solution(7533915594061974568)
XLA Ops:
  1.3 1.3 %broadcast_in_dim.7.prec = f32[1,4800]{1,0:T(1,128)} reshape(f32[4800]{0:T(1024)} %param.9) | data formatting | bytes 38400 | tf_op jit(solution)/shard_map/broadcast_in_dim | solution.py:388
  2.6 39.0 %shard_map.85 = (f32[1,256]{1,0:T(1,128)}, f32[1,256]{1,0:T(1,128)}, f32[256,128]{1,0:T(8,128)}) custom-call(bf16[32,64,256]{2,1,0:T(8,128)(2,1)} %jac.1, f32[32,64]{1,0:T(8,128)} %meas.1, s32[1,32]{1,0:T(1,128)} %bitcast.5, f32[1,4800]{1,0:T(1,128)} %broadcast_in_dim.7.prec, s32[1]{0:T(128)S(6)} %copy.12.live, f32[5,1024]{1,0:T(8,128)} %ret.1), custom_call_target="tpu_custom_call" | custom-call | tf_op jit(solution)/shard_map/pallas_call | solution.py:356
  41.7 0.0 copy-start.1
  41.7 0.6 %copy-done.1 = f32[1,256]{1,0:T(1,128)S(1)} copy-done((f32[1,256]{1,0:T(1,128)S(1)}, f32[1,256]{1,0:T(1,128)}, u32[]{:S(2)}) %copy-start.1) | copy-done | bytes 1048
  42.3 0.0 copy-start
  42.3 0.6 %copy.13 = f32[256]{0:T(256)} copy(f32[256]{0:T(256)S(1)} %bitcast.4) | data formatting | bytes 2048
  42.9 0.1 copy-done
  43.0 0.6 %copy.14 = f32[256]{0:T(256)} copy(f32[256]{0:T(256)S(1)} %bitcast.3) | data formatting | bytes 2048
  43.5 1.6 %copy.15 = f32[256,128]{1,0:T(8,128)} copy(f32[256,128]{1,0:T(8,128)} %get-tuple-element.14) | data formatting | bytes 262144
Async XLA Ops:
  41.7 0.6 %copy-start.1 = (f32[1,256]{1,0:T(1,128)S(1)}, f32[1,256]{1,0:T(1,128)}, u32[]{:S(2)}) copy-start(f32[1,256]{1,0:T(1,128)} %get-tuple-element.6) | copy-start | bytes 3076
  42.3 0.7 %copy-start = (f32[1,256]{1,0:T(1,128)S(1)}, f32[1,256]{1,0:T(1,128)}, u32[]{:S(2)}) copy-start(f32[1,256]{1,0:T(1,128)} %get-tuple-element.7) | copy-start | bytes 3076
